TPU v7x, 128 devices: a whole 4x4x4 slice. The times are simulated.
128 devices in a mesh: seq: 32 (over x, y, core), trk: 4 (over z).
Axes of the slice: x: 4, y: 4, z: 4, core: 2. Of those that a mesh axis runs over, the one named last changes fastest.
Arguments:
- trunk_input: bfloat16 [12288, 1536], P('seq', 'trk'), may hold values from -6 to 6
- conv_in: bfloat16 [6, 3, 768, 1536], P(None, None, 'trk'), may hold values from -0.09375 to 0.09375
- conv_bias: bfloat16 [6, 768], P(None, 'trk'), may hold values from -3 to 3
- conv_out: bfloat16 [6, 768, 1536], P(None, 'trk'), may hold values from -0.21875 to 0.21875
- projection_bias: bfloat16 [6, 1536], P(None, 'trk'), may hold values from -3 to 3
- head_weight: bfloat16 [1536, 4096], P(None, 'trk'), may hold values from -0.15625 to 0.15625
- head_bias: bfloat16 [4096], P('trk'), may hold values from -4 to 4
- exon_bins: int32 [256, 64], P('seq'), may hold values from -1 to 12287, as said below
Outputs:
- coverage: bfloat16 [12288, 4096], P('seq', 'trk')
- gene_cov: float32 [256, 4096], P('seq', 'trk')
Inputs may be any that keep to these rules, and one draw needn't show every extreme that they name: `exon_bins`: row g lists gene g's exon bins in increasing order, then -1 in the unused entries; every gene has at least one exon bin and some gene has exactly 64. The genes of rows 8 * o to 8 * (o + 1) - 1 are owned by index o of seq.
All inputs are finite; a program needn't handle non-finite values.
Results may differ from a plain program's by a relative error of at most 0.024.
Values may be sent and summed in bfloat16 or wider, within the bound.
A program may use at most 128 MiB of HBM per device.

v0:
```python
import jax
import jax.numpy as jnp
from jax import lax
from jax.sharding import PartitionSpec as P

RESIDUAL_BLOCKS = 6
BASE_DILATION = 2


def extended(cells, sides, width):
    for axis, dim in sides:
        count = lax.axis_size(axis)
        ends = count - 1
        head = lax.slice_in_dim(cells, 0, width, axis=dim)
        tail = lax.slice_in_dim(cells, cells.shape[dim] - width, cells.shape[dim], axis=dim)
        cells = jnp.concatenate(
            [
                lax.ppermute(tail, axis, [(i, (i + 1) % count) for i in range(ends)]),
                cells,
                lax.ppermute(head, axis, [((i + 1) % count, i) for i in range(ends)]),
            ],
            axis=dim,
        )
    return cells


def contract_last(rows, kernel):
    return lax.dot_general(
        rows, kernel, (((1,), (1,)), ((), ())), preferred_element_type=jnp.float32
    )


def dilated_inner(trunk, conv_in, block_layer_index, dilation_step):
    bin_rows = trunk.shape[0]
    gathered = lax.all_gather(trunk, "trk", axis=1, tiled=True)
    padded = extended(gathered, (("seq", 0),), dilation_step)
    inner = jnp.zeros((bin_rows, conv_in.shape[2]), jnp.float32)
    for tap_index in range(3):
        window = padded[tap_index * dilation_step : tap_index * dilation_step + bin_rows]
        inner = inner + contract_last(window, conv_in[block_layer_index, tap_index])
    return inner


def exon_onehot(gene_block, width_now):
    exon_matches = gene_block[:, :, None] == jnp.arange(width_now, dtype=jnp.int32)[None, None, :]
    return jnp.sum(exon_matches.astype(jnp.float32), axis=1).astype(jnp.bfloat16)


def shards(
    trunk_input, conv_in, conv_bias, conv_out, projection_bias, head_weight, head_bias, exon_bins
):
    trunk = trunk_input
    for block_layer_index in range(RESIDUAL_BLOCKS):
        dilation_step = BASE_DILATION * 2**block_layer_index
        inner = dilated_inner(trunk, conv_in, block_layer_index, dilation_step)
        activation = jax.nn.gelu(
            inner + conv_bias[block_layer_index].astype(jnp.float32), approximate=True
        ).astype(jnp.bfloat16)
        partial_value = jnp.dot(
            activation, conv_out[block_layer_index], preferred_element_type=jnp.float32
        )
        summed = lax.psum_scatter(
            partial_value.astype(jnp.bfloat16), "trk", scatter_dimension=1, tiled=True
        ).astype(jnp.float32)
        trunk = (
            trunk.astype(jnp.float32)
            + summed
            + projection_bias[block_layer_index].astype(jnp.float32)
        ).astype(jnp.bfloat16)
    logits = jnp.dot(
        lax.all_gather(trunk, "trk", axis=1, tiled=True),
        head_weight,
        preferred_element_type=jnp.float32,
    )
    coverage = jax.nn.softplus(logits + head_bias.astype(jnp.float32)).astype(jnp.bfloat16)
    shard_rows = lax.all_gather(coverage, "seq", axis=0, tiled=True)
    onehot = exon_onehot(exon_bins, shard_rows.shape[0])
    gene_sum = jnp.dot(onehot, shard_rows, preferred_element_type=jnp.float32)
    counts = jnp.sum((exon_bins >= 0).astype(jnp.float32), axis=1)
    gene_cov = gene_sum / counts[:, None]
    return (coverage, gene_cov)


def solution(mesh):
    in_specs = (
        P("seq", "trk"),
        P(None, None, "trk", None),
        P(None, "trk"),
        P(None, "trk", None),
        P(None, "trk"),
        P(None, "trk"),
        P("trk"),
        P("seq", None),
    )
    out_specs = (P("seq", "trk"), P("seq", "trk"))
    return jax.shard_map(shards, mesh=mesh, in_specs=in_specs, out_specs=out_specs, check_vma=False)
```

profile of v0, /device:TPU:1, one launch (start us, length us, event | category | flops | bytes accessed | tf_op | source)
XLA Modules:
  0.0 589.5 jit_solution(15093628703576068689)
XLA Ops:
  8.9 26.9 %all-gather.9.cloned.1.call-done = bf16[384,1536]{1,0:T(8,128)(2,1)} async-done(((bf16[384,384]{1,0:T(8,128)(2,1)}), bf16[384,1536]{1,0:T(8,128)(2,1)}) %all-gather.9.cloned.1.call-update) | async-done | bytes 1179664 | tf_op jit(solution)/shard_map/all_gather | solution.py:35
  36.6 6.0 %collective-permute-start = (bf16[2,1536]{1,0:T(2,128)(2,1)S(1)}, bf16[2,1536]{1,0:T(2,128)(2,1)S(1)}, u32[]{:S(2)}, u32[]{:S(2)}) collective-permute-start(bf16[2,1536]{1,0:T(2,128)(2,1)S(1)} %get-tuple-element.18), channel_id=1, source_target_pairs={{0,4},{4,8},{8,12},{12,16},{16,20},{20,24},{24,28},{28,32},{32,36}... | collective-permute-start | bytes 18440 | tf_op jit(solution)/shard_map/ppermute | solution.py:18
  49.9 3.9 convolution_convert_fusion.5
  56.9 23.2 %reduce-scatter.19.cloned.1.call-done = bf16[384,384]{1,0:T(8,128)(2,1)} async-done(((bf16[1536,384]{1,0:T(8,128)(2,1)}), bf16[384,384]{1,0:T(8,128)(2,1)}) %reduce-scatter.19.cloned.1.call-update) | async-done | bytes 294928
  83.8 24.2 %all-gather.11.cloned.1.call-done = bf16[384,1536]{1,0:T(8,128)(2,1)} async-done(((bf16[384,384]{1,0:T(8,128)(2,1)}), bf16[384,1536]{1,0:T(8,128)(2,1)}) %all-gather.11.cloned.1.call-update) | async-done | bytes 1179664 | tf_op jit(solution)/shard_map/all_gather | solution.py:35
  108.9 6.0 %collective-permute-start.2 = (bf16[4,1536]{1,0:T(4,128)(2,1)S(1)}, bf16[4,1536]{1,0:T(4,128)(2,1)S(1)}, u32[]{:S(2)}, u32[]{:S(2)}) collective-permute-start(bf16[4,1536]{1,0:T(4,128)(2,1)S(1)} %get-tuple-element.16), channel_id=1, source_target_pairs={{0,4},{4,8},{8,12},{12,16},{16,20},{20,24},{24,28},{28,32},{32,36}... | collective-permute-start | bytes 36872 | tf_op jit(solution)/shard_map/ppermute | solution.py:18
  116.8 2.7 fusion.65
  122.2 4.0 convolution_convert_fusion.4
  128.7 23.4 %reduce-scatter.21.cloned.1.call-done = bf16[384,384]{1,0:T(8,128)(2,1)} async-done(((bf16[1536,384]{1,0:T(8,128)(2,1)}), bf16[384,384]{1,0:T(8,128)(2,1)}) %reduce-scatter.21.cloned.1.call-update) | async-done | bytes 294928
  155.8 24.6 %all-gather.13.cloned.1.call-done = bf16[384,1536]{1,0:T(8,128)(2,1)} async-done(((bf16[384,384]{1,0:T(8,128)(2,1)}), bf16[384,1536]{1,0:T(8,128)(2,1)}) %all-gather.13.cloned.1.call-update) | async-done | bytes 1179664 | tf_op jit(solution)/shard_map/all_gather | solution.py:35
  181.2 6.0 %collective-permute-start.4 = (bf16[8,1536]{1,0:T(8,128)(2,1)S(1)}, bf16[8,1536]{1,0:T(8,128)(2,1)S(1)}, u32[]{:S(2)}, u32[]{:S(2)}) collective-permute-start(bf16[8,1536]{1,0:T(8,128)(2,1)S(1)} %get-tuple-element.14), channel_id=1, source_target_pairs={{0,4},{4,8},{8,12},{12,16},{16,20},{20,24},{24,28},{28,32},{32,36}... | collective-permute-start | bytes 73736 | tf_op jit(solution)/shard_map/ppermute | solution.py:18
  189.2 2.7 fusion.60
  194.7 4.0 convolution_convert_fusion.3
  201.1 23.8 %reduce-scatter.23.cloned.1.call-done = bf16[384,384]{1,0:T(8,128)(2,1)} async-done(((bf16[1536,384]{1,0:T(8,128)(2,1)}), bf16[384,384]{1,0:T(8,128)(2,1)}) %reduce-scatter.23.cloned.1.call-update) | async-done | bytes 294928
  228.6 24.2 %all-gather.15.cloned.1.call-done = bf16[384,1536]{1,0:T(8,128)(2,1)} async-done(((bf16[384,384]{1,0:T(8,128)(2,1)}), bf16[384,1536]{1,0:T(8,128)(2,1)}) %all-gather.15.cloned.1.call-update) | async-done | bytes 1179664 | tf_op jit(solution)/shard_map/all_gather | solution.py:35
  253.7 6.0 %collective-permute-start.6 = (bf16[16,1536]{1,0:T(8,128)(2,1)S(1)}, bf16[16,1536]{1,0:T(8,128)(2,1)S(1)}, u32[]{:S(2)}, u32[]{:S(2)}) collective-permute-start(bf16[16,1536]{1,0:T(8,128)(2,1)S(1)} %get-tuple-element.12), channel_id=1, source_target_pairs={{0,4},{4,8},{8,12},{12,16},{16,20},{20,24},{24,28},{28,32},{32,36}... | collective-permute-start | bytes 147464 | tf_op jit(solution)/shard_map/ppermute | solution.py:18
  261.6 2.7 fusion.55
  267.5 3.9 convolution_convert_fusion.2
  273.9 23.8 %reduce-scatter.25.cloned.1.call-done = bf16[384,384]{1,0:T(8,128)(2,1)} async-done(((bf16[1536,384]{1,0:T(8,128)(2,1)}), bf16[384,384]{1,0:T(8,128)(2,1)}) %reduce-scatter.25.cloned.1.call-update) | async-done | bytes 294928
  301.3 24.2 %all-gather.17.cloned.1.call-done = bf16[384,1536]{1,0:T(8,128)(2,1)} async-done(((bf16[384,384]{1,0:T(8,128)(2,1)}), bf16[384,1536]{1,0:T(8,128)(2,1)}) %all-gather.17.cloned.1.call-update) | async-done | bytes 1179664 | tf_op jit(solution)/shard_map/all_gather | solution.py:35
  326.5 6.1 %collective-permute-start.8 = (bf16[32,1536]{1,0:T(8,128)(2,1)S(1)}, bf16[32,1536]{1,0:T(8,128)(2,1)S(1)}, u32[]{:S(2)}, u32[]{:S(2)}) collective-permute-start(bf16[32,1536]{1,0:T(8,128)(2,1)S(1)} %get-tuple-element.10), channel_id=1, source_target_pairs={{0,4},{4,8},{8,12},{12,16},{16,20},{20,24},{24,28},{28,32},{32,36}... | collective-permute-start | bytes 294920 | tf_op jit(solution)/shard_map/ppermute | solution.py:18
  340.9 3.9 convolution_convert_fusion.1
  347.3 23.6 %reduce-scatter.27.cloned.1.call-done = bf16[384,384]{1,0:T(8,128)(2,1)} async-done(((bf16[1536,384]{1,0:T(8,128)(2,1)}), bf16[384,384]{1,0:T(8,128)(2,1)}) %reduce-scatter.27.cloned.1.call-update) | async-done | bytes 294928
  374.6 24.4 %all-gather.19.cloned.1.call-done = bf16[384,1536]{1,0:T(8,128)(2,1)} async-done(((bf16[384,384]{1,0:T(8,128)(2,1)}), bf16[384,1536]{1,0:T(8,128)(2,1)}) %all-gather.19.cloned.1.call-update) | async-done | bytes 1179664 | tf_op jit(solution)/shard_map/all_gather | solution.py:35
  400.1 6.1 %collective-permute-start.10 = (bf16[64,1536]{1,0:T(8,128)(2,1)S(1)}, bf16[64,1536]{1,0:T(8,128)(2,1)S(1)}, u32[]{:S(2)}, u32[]{:S(2)}) collective-permute-start(bf16[64,1536]{1,0:T(8,128)(2,1)S(1)} %get-tuple-element.8), channel_id=1, source_target_pairs={{0,4},{4,8},{8,12},{12,16},{16,20},{20,24},{24,28},{28,32},{32,36}... | collective-permute-start | bytes 589832 | tf_op jit(solution)/shard_map/ppermute | solution.py:18
  415.5 3.9 convolution_convert_fusion
  421.9 23.4 %reduce-scatter.29.cloned.1.call-done = bf16[384,384]{1,0:T(8,128)(2,1)} async-done(((bf16[1536,384]{1,0:T(8,128)(2,1)}), bf16[384,384]{1,0:T(8,128)(2,1)}) %reduce-scatter.29.cloned.1.call-update) | async-done | bytes 294928
  449.0 24.6 %all-gather.21.cloned.1.call-done = bf16[384,1536]{1,0:T(8,128)(2,1)} async-done(((bf16[384,384]{1,0:T(8,128)(2,1)}), bf16[384,1536]{1,0:T(8,128)(2,1)}) %all-gather.21.cloned.1.call-update) | async-done | bytes 1179664 | tf_op jit(solution)/shard_map/all_gather | solution.py:71
  473.6 4.2 fusion
  478.0 4.9 convert_reduce_fusion
  482.9 89.5 %all-gather.23.cloned.1.call-done = bf16[12288,1024]{1,0:T(8,128)(2,1)} async-done(((bf16[384,1024]{1,0:T(8,128)(2,1)}), bf16[12288,1024]{1,0:T(8,128)(2,1)}) %all-gather.23.cloned.1.call-update) | async-done | bytes 25165840 | tf_op jit(solution)/shard_map/all_gather | solution.py:76
  572.4 10.5 %convolution_divide_fusion = f32[8,1024]{1,0:T(8,128)} fusion(bf16[12288,1024]{1,0:T(8,128)(2,1)} %all-gather.23.cloned.1.call-done, bf16[8,12288]{1,0:T(8,128)(2,1)S(1)} %convert_reduce_fusion, f32[8]{0:T(128)S(1)} %convert_reduce_fusion.1), kind=kOutput, calls=%fused_computation.64 | convolution fusion | flops 201334784 | bytes 25395232 | tf_op jit(solution)/shard_map/dot_general | solution.py:78
  (115 shorter events, 84.1 us)
Async XLA Ops:
  7.2 466.5 %copy-start = (bf16[1536,1024]{1,0:T(8,128)(2,1)S(1)}, bf16[1536,1024]{1,0:T(8,128)(2,1)}, u32[]{:S(2)}) copy-start(bf16[1536,1024]{1,0:T(8,128)(2,1)} %param.13) | copy-start | bytes 9437188
  7.2 28.6 %all-gather.9.cloned.1.call-start = ((), (), s32[]{:S(2)}) async-start(), calls=%async_computation.6 | async-start | bytes 1474560 | tf_op jit(solution)/shard_map/all_gather | solution.py:35
  7.9 72.2 %reduce-scatter.19.cloned.1.call-start = ((), (), s32[]{:S(2)}) async-start(), calls=%async_computation.14 | async-start | bytes 1474560
  36.6 13.3 %collective-permute-start = (bf16[2,1536]{1,0:T(2,128)(2,1)S(1)}, bf16[2,1536]{1,0:T(2,128)(2,1)S(1)}, u32[]{:S(2)}, u32[]{:S(2)}) collective-permute-start(bf16[2,1536]{1,0:T(2,128)(2,1)S(1)} %get-tuple-element.18), channel_id=1, source_target_pairs={{0,4},{4,8},{8,12},{12,16},{16,20},{20,24},{24,28},{28,32},{32,36}... | collective-permute-start | bytes 18440 | tf_op jit(solution)/shard_map/ppermute | solution.py:18
  42.6 4.9 collective-permute-start.1
  56.2 25.8 %copy-start.6 = (bf16[384,384]{1,0:T(8,128)(2,1)S(1)}, bf16[384,384]{1,0:T(8,128)(2,1)}, u32[]{:S(2)}) copy-start(bf16[384,384]{1,0:T(8,128)(2,1)} %param.8) | copy-start | bytes 884740
  56.2 51.8 %all-gather.11.cloned.1.call-start = ((), (), s32[]{:S(2)}) async-start(), calls=%async_computation.7 | async-start | bytes 1474560 | tf_op jit(solution)/shard_map/all_gather | solution.py:35
  83.8 68.3 %reduce-scatter.21.cloned.1.call-start = ((), (), s32[]{:S(2)}) async-start(), calls=%async_computation.15 | async-start | bytes 1474560
  108.9 13.4 %collective-permute-start.2 = (bf16[4,1536]{1,0:T(4,128)(2,1)S(1)}, bf16[4,1536]{1,0:T(4,128)(2,1)S(1)}, u32[]{:S(2)}, u32[]{:S(2)}) collective-permute-start(bf16[4,1536]{1,0:T(4,128)(2,1)S(1)} %get-tuple-element.16), channel_id=1, source_target_pairs={{0,4},{4,8},{8,12},{12,16},{16,20},{20,24},{24,28},{28,32},{32,36}... | collective-permute-start | bytes 36872 | tf_op jit(solution)/shard_map/ppermute | solution.py:18
  114.9 5.0 collective-permute-start.3
  128.6 51.8 %all-gather.13.cloned.1.call-start = ((), (), s32[]{:S(2)}) async-start(), calls=%async_computation.8 | async-start | bytes 1474560 | tf_op jit(solution)/shard_map/all_gather | solution.py:35
  155.7 69.2 %reduce-scatter.23.cloned.1.call-start = ((), (), s32[]{:S(2)}) async-start(), calls=%async_computation.16 | async-start | bytes 1474560
  181.2 13.5 %collective-permute-start.4 = (bf16[8,1536]{1,0:T(8,128)(2,1)S(1)}, bf16[8,1536]{1,0:T(8,128)(2,1)S(1)}, u32[]{:S(2)}, u32[]{:S(2)}) collective-permute-start(bf16[8,1536]{1,0:T(8,128)(2,1)S(1)} %get-tuple-element.14), channel_id=1, source_target_pairs={{0,4},{4,8},{8,12},{12,16},{16,20},{20,24},{24,28},{28,32},{32,36}... | collective-permute-start | bytes 73736 | tf_op jit(solution)/shard_map/ppermute | solution.py:18
  187.2 5.1 collective-permute-start.5
  201.1 25.7 %copy-start.2 = (bf16[384,384]{1,0:T(8,128)(2,1)S(1)}, bf16[384,384]{1,0:T(8,128)(2,1)}, u32[]{:S(2)}) copy-start(bf16[384,384]{1,0:T(8,128)(2,1)} %add_convert_fusion.4) | copy-start | bytes 884740
  201.1 51.7 %all-gather.15.cloned.1.call-start = ((), (), s32[]{:S(2)}) async-start(), calls=%async_computation.9 | async-start | bytes 1474560 | tf_op jit(solution)/shard_map/all_gather | solution.py:35
  228.6 69.1 %reduce-scatter.25.cloned.1.call-start = ((), (), s32[]{:S(2)}) async-start(), calls=%async_computation.17 | async-start | bytes 1474560
  253.7 13.7 %collective-permute-start.6 = (bf16[16,1536]{1,0:T(8,128)(2,1)S(1)}, bf16[16,1536]{1,0:T(8,128)(2,1)S(1)}, u32[]{:S(2)}, u32[]{:S(2)}) collective-permute-start(bf16[16,1536]{1,0:T(8,128)(2,1)S(1)} %get-tuple-element.12), channel_id=1, source_target_pairs={{0,4},{4,8},{8,12},{12,16},{16,20},{20,24},{24,28},{28,32},{32,36}... | collective-permute-start | bytes 147464 | tf_op jit(solution)/shard_map/ppermute | solution.py:18
  259.7 5.4 collective-permute-start.7
  273.8 25.7 %copy-start.3 = (bf16[384,384]{1,0:T(8,128)(2,1)S(1)}, bf16[384,384]{1,0:T(8,128)(2,1)}, u32[]{:S(2)}) copy-start(bf16[384,384]{1,0:T(8,128)(2,1)} %add_convert_fusion.3) | copy-start | bytes 884740
  273.8 51.7 %all-gather.17.cloned.1.call-start = ((), (), s32[]{:S(2)}) async-start(), calls=%async_computation.10 | async-start | bytes 1474560 | tf_op jit(solution)/shard_map/all_gather | solution.py:35
  301.3 69.6 %reduce-scatter.27.cloned.1.call-start = ((), (), s32[]{:S(2)}) async-start(), calls=%async_computation.18 | async-start | bytes 1474560
  326.5 14.4 %collective-permute-start.8 = (bf16[32,1536]{1,0:T(8,128)(2,1)S(1)}, bf16[32,1536]{1,0:T(8,128)(2,1)S(1)}, u32[]{:S(2)}, u32[]{:S(2)}) collective-permute-start(bf16[32,1536]{1,0:T(8,128)(2,1)S(1)} %get-tuple-element.10), channel_id=1, source_target_pairs={{0,4},{4,8},{8,12},{12,16},{16,20},{20,24},{24,28},{28,32},{32,36}... | collective-permute-start | bytes 294920 | tf_op jit(solution)/shard_map/ppermute | solution.py:18
  332.7 5.9 %collective-permute-start.9 = (bf16[32,1536]{1,0:T(8,128)(2,1)S(1)}, bf16[32,1536]{1,0:T(8,128)(2,1)S(1)}, u32[]{:S(2)}, u32[]{:S(2)}) collective-permute-start(bf16[32,1536]{1,0:T(8,128)(2,1)S(1)} %get-tuple-element.11), channel_id=1, source_target_pairs={{4,0},{8,4},{12,8},{16,12},{20,16},{24,20},{28,24},{32,28},{36,32}... | collective-permute-start | bytes 294920 | tf_op jit(solution)/shard_map/ppermute | solution.py:20
  347.3 51.7 %all-gather.19.cloned.1.call-start = ((), (), s32[]{:S(2)}) async-start(), calls=%async_computation.11 | async-start | bytes 1474560 | tf_op jit(solution)/shard_map/all_gather | solution.py:35
  374.5 70.8 %reduce-scatter.29.cloned.1.call-start = ((), (), s32[]{:S(2)}) async-start(), calls=%async_computation.19 | async-start | bytes 1474560
  400.1 15.5 %collective-permute-start.10 = (bf16[64,1536]{1,0:T(8,128)(2,1)S(1)}, bf16[64,1536]{1,0:T(8,128)(2,1)S(1)}, u32[]{:S(2)}, u32[]{:S(2)}) collective-permute-start(bf16[64,1536]{1,0:T(8,128)(2,1)S(1)} %get-tuple-element.8), channel_id=1, source_target_pairs={{0,4},{4,8},{8,12},{12,16},{16,20},{20,24},{24,28},{28,32},{32,36}... | collective-permute-start | bytes 589832 | tf_op jit(solution)/shard_map/ppermute | solution.py:18
  406.2 7.0 %collective-permute-start.11 = (bf16[64,1536]{1,0:T(8,128)(2,1)S(1)}, bf16[64,1536]{1,0:T(8,128)(2,1)S(1)}, u32[]{:S(2)}, u32[]{:S(2)}) collective-permute-start(bf16[64,1536]{1,0:T(8,128)(2,1)S(1)} %get-tuple-element.9), channel_id=1, source_target_pairs={{4,0},{8,4},{12,8},{16,12},{20,16},{24,20},{28,24},{32,28},{36,32}... | collective-permute-start | bytes 589832 | tf_op jit(solution)/shard_map/ppermute | solution.py:20
  421.8 27.1 %copy-start.12 = (bf16[1024]{0:T(1024)(128)(2,1)S(1)}, bf16[1024]{0:T(1024)(128)(2,1)}, u32[]{:S(2)}) copy-start(bf16[1024]{0:T(1024)(128)(2,1)} %param.14) | copy-start | bytes 6148
  421.9 51.8 %all-gather.21.cloned.1.call-start = ((), (), s32[]{:S(2)}) async-start(), calls=%async_computation.12 | async-start | bytes 1474560 | tf_op jit(solution)/shard_map/all_gather | solution.py:71
  448.9 123.5 %all-gather.23.cloned.1.call-start = ((), (), s32[]{:S(2)}) async-start(), calls=%async_computation.13 | async-start | bytes 25952256 | tf_op jit(solution)/shard_map/all_gather | solution.py:76
  449.0 28.9 %copy-start.9 = (s32[8,64]{1,0:T(8,128)S(1)}, s32[8,64]{1,0:T(8,128)}, u32[]{:S(2)}) copy-start(s32[8,64]{1,0:T(8,128)} %param.15) | copy-start | bytes 6148
  (10 other events, 150.0 us)
Sparse Core Ops, SparseCore 0:
  9.7 26.0 all-gather.8
  56.3 23.7 reduce-scatter.18
  83.9 24.0 all-gather.10
  128.7 23.2 reduce-scatter.20
  155.8 24.5 all-gather.12
  201.2 23.6 reduce-scatter.22
  228.7 24.0 all-gather.14
  273.9 23.6 reduce-scatter.24
  301.4 24.1 all-gather.16
  347.4 23.4 reduce-scatter.26
  374.7 24.3 all-gather.18
  422.0 23.2 reduce-scatter.28
  449.1 24.5 all-gather.20
  478.0 94.4 all-gather.22
where the time goes:
time: 591 us; the launch traced here: 589 us
  waiting for transfers between devices  411 us (70%)
  matrix products  67.8 us (11%)
  starting transfers between devices  48.4 us (8%)
  local copies, waits for them, and re-layouts  31.5 us (5%)
  other arithmetic  16.6 us (3%)
  between operations  14.2 us (2%)
    all_gather x6, waiting for transfers between devices, dilated_inner(): gathered = lax.all_gather(trunk, 'trk', axis=1, tiled=True)  149 us
    unnamed x20, waiting for transfers between devices  142 us
    all_gather x1, waiting for transfers between devices, shards(): shard_rows = lax.all_gather(coverage, 'seq', axis=0, tiled=True)  89.5 us
    ppermute x6, starting transfers between devices, extended(): lax.ppermute(tail, axis, [(i, (i + 1) % count) for i in range(ends)])  36.1 us
    dot_general x12, matrix products, contract_last(): lax.dot_general(rows, kernel, (((1,), (1,)), ((), ())), preferred_element...  29.5 us
    unnamed x44, local copies, waits for them, and re-layouts  26 us
    all_gather x1, waiting for transfers between devices, shards(): lax.all_gather(trunk, 'trk', axis=1, tiled=True)  24.6 us
    dot_general x6, matrix products, shards(): jnp.dot(activation, conv_out[block_layer_index], preferred_element_type=j...  23.6 us
  transfers between devices with their start and end apart: 26, of which 20 were waited for; matrix products, arithmetic and copies ran while one was open for 6% of the time, Pallas kernels for 0%

commit v1 on v0

--- a/solution.py
+++ b/solution.py
@@ -73,7 +73,10 @@
         preferred_element_type=jnp.float32,
     )
     coverage = jax.nn.softplus(logits + head_bias.astype(jnp.float32)).astype(jnp.bfloat16)
-    shard_rows = lax.all_gather(coverage, "seq", axis=0, tiled=True)
+    n_dev = lax.axis_size("seq")
+    blocks = jnp.stack([coverage for _ in range(n_dev)])
+    blocks = lax.all_to_all(blocks, "seq", split_axis=0, concat_axis=0)
+    shard_rows = jnp.concatenate(blocks, axis=0)
     onehot = exon_onehot(exon_bins, shard_rows.shape[0])
     gene_sum = jnp.dot(onehot, shard_rows, preferred_element_type=jnp.float32)
     counts = jnp.sum((exon_bins >= 0).astype(jnp.float32), axis=1)

time: 591 us -> 912 us (1.54)
  the two profiles are of different devices: /device:TPU:1 before, /device:TPU:12 now
where the time goes in v1:
time: 912 us; the launch traced here: 910 us
  waiting for transfers between devices  736 us (81%)
  matrix products  67.1 us (7%)
  local copies, waits for them, and re-layouts  41 us (4%)
  starting transfers between devices  34.5 us (4%)
  other arithmetic  16.6 us (2%)
  between operations  14.2 us (2%)
    all_to_all x1, waiting for transfers between devices, shards(): blocks = lax.all_to_all(blocks, 'seq', split_axis=0, concat_axis=0)  405 us
    unnamed x19, waiting for transfers between devices  153 us
    all_gather x6, waiting for transfers between devices, dilated_inner(): gathered = lax.all_gather(trunk, 'trk', axis=1, tiled=True)  153 us
    dot_general x12, matrix products, contract_last(): lax.dot_general(rows, kernel, (((1,), (1,)), ((), ())), preferred_element...  29.5 us
    unnamed x48, local copies, waits for them, and re-layouts  26.8 us
    all_gather x1, waiting for transfers between devices, shards(): lax.all_gather(trunk, 'trk', axis=1, tiled=True)  24.9 us
    dot_general x6, matrix products, shards(): jnp.dot(activation, conv_out[block_layer_index], preferred_element_type=j...  23.7 us
  transfers between devices with their start and end apart: 26, of which 14 were waited for; matrix products, arithmetic and copies ran while one was open for 4% of the time, Pallas kernels for 0%

profile of v1, /device:TPU:12, one launch (start us, length us, event | category | flops | bytes accessed | tf_op | source)
XLA Modules:
  0.0 909.8 jit_solution(13743148819214285229)
XLA Ops:
  8.9 28.2 %all-gather.8.cloned.1.call-done = bf16[384,1536]{1,0:T(8,128)(2,1)} async-done(((bf16[384,384]{1,0:T(8,128)(2,1)}), bf16[384,1536]{1,0:T(8,128)(2,1)}) %all-gather.8.cloned.1.call-update) | async-done | bytes 1179664 | tf_op jit(solution)/shard_map/all_gather | solution.py:35
  39.9 2.4 collective-permute-start
  46.7 3.9 convolution_convert_fusion.5
  53.7 24.9 %reduce-scatter.19.cloned.1.call-done = bf16[384,384]{1,0:T(8,128)(2,1)} async-done(((bf16[1536,384]{1,0:T(8,128)(2,1)}), bf16[384,384]{1,0:T(8,128)(2,1)}) %reduce-scatter.19.cloned.1.call-update) | async-done | bytes 294928
  82.3 24.9 %all-gather.10.cloned.1.call-done = bf16[384,1536]{1,0:T(8,128)(2,1)} async-done(((bf16[384,384]{1,0:T(8,128)(2,1)}), bf16[384,1536]{1,0:T(8,128)(2,1)}) %all-gather.10.cloned.1.call-update) | async-done | bytes 1179664 | tf_op jit(solution)/shard_map/all_gather | solution.py:35
  112.3 2.7 fusion.65
  117.4 4.0 convolution_convert_fusion.4
  123.8 25.5 %reduce-scatter.21.cloned.1.call-done = bf16[384,384]{1,0:T(8,128)(2,1)} async-done(((bf16[1536,384]{1,0:T(8,128)(2,1)}), bf16[384,384]{1,0:T(8,128)(2,1)}) %reduce-scatter.21.cloned.1.call-update) | async-done | bytes 294928
  153.1 24.9 %all-gather.12.cloned.1.call-done = bf16[384,1536]{1,0:T(8,128)(2,1)} async-done(((bf16[384,384]{1,0:T(8,128)(2,1)}), bf16[384,1536]{1,0:T(8,128)(2,1)}) %all-gather.12.cloned.1.call-update) | async-done | bytes 1179664 | tf_op jit(solution)/shard_map/all_gather | solution.py:35
  183.1 2.7 fusion.60
  188.1 4.0 convolution_convert_fusion.3
  194.6 25.6 %reduce-scatter.23.cloned.1.call-done = bf16[384,384]{1,0:T(8,128)(2,1)} async-done(((bf16[1536,384]{1,0:T(8,128)(2,1)}), bf16[384,384]{1,0:T(8,128)(2,1)}) %reduce-scatter.23.cloned.1.call-update) | async-done | bytes 294928
  223.8 24.8 %all-gather.14.cloned.1.call-done = bf16[384,1536]{1,0:T(8,128)(2,1)} async-done(((bf16[384,384]{1,0:T(8,128)(2,1)}), bf16[384,1536]{1,0:T(8,128)(2,1)}) %all-gather.14.cloned.1.call-update) | async-done | bytes 1179664 | tf_op jit(solution)/shard_map/all_gather | solution.py:35
  253.9 2.7 fusion.55
  258.9 4.0 convolution_convert_fusion.2
  265.4 25.5 %reduce-scatter.25.cloned.1.call-done = bf16[384,384]{1,0:T(8,128)(2,1)} async-done(((bf16[1536,384]{1,0:T(8,128)(2,1)}), bf16[384,384]{1,0:T(8,128)(2,1)}) %reduce-scatter.25.cloned.1.call-update) | async-done | bytes 294928
  294.6 24.9 %all-gather.16.cloned.1.call-done = bf16[384,1536]{1,0:T(8,128)(2,1)} async-done(((bf16[384,384]{1,0:T(8,128)(2,1)}), bf16[384,1536]{1,0:T(8,128)(2,1)}) %all-gather.16.cloned.1.call-update) | async-done | bytes 1179664 | tf_op jit(solution)/shard_map/all_gather | solution.py:35
  322.5 2.6 collective-permute-start.8
  325.1 2.7 fusion.50
  330.1 3.9 convolution_convert_fusion.1
  336.5 25.5 %reduce-scatter.27.cloned.1.call-done = bf16[384,384]{1,0:T(8,128)(2,1)} async-done(((bf16[1536,384]{1,0:T(8,128)(2,1)}), bf16[384,384]{1,0:T(8,128)(2,1)}) %reduce-scatter.27.cloned.1.call-update) | async-done | bytes 294928
  365.7 24.9 %all-gather.18.cloned.1.call-done = bf16[384,1536]{1,0:T(8,128)(2,1)} async-done(((bf16[384,384]{1,0:T(8,128)(2,1)}), bf16[384,1536]{1,0:T(8,128)(2,1)}) %all-gather.18.cloned.1.call-update) | async-done | bytes 1179664 | tf_op jit(solution)/shard_map/all_gather | solution.py:35
  396.1 2.7 fusion.45
  401.2 3.9 convolution_convert_fusion
  407.5 25.5 %reduce-scatter.29.cloned.1.call-done = bf16[384,384]{1,0:T(8,128)(2,1)} async-done(((bf16[1536,384]{1,0:T(8,128)(2,1)}), bf16[384,384]{1,0:T(8,128)(2,1)}) %reduce-scatter.29.cloned.1.call-update) | async-done | bytes 294928
  436.7 24.9 %all-gather.20.cloned.1.call-done = bf16[384,1536]{1,0:T(8,128)(2,1)} async-done(((bf16[384,384]{1,0:T(8,128)(2,1)}), bf16[384,1536]{1,0:T(8,128)(2,1)}) %all-gather.20.cloned.1.call-update) | async-done | bytes 1179664 | tf_op jit(solution)/shard_map/all_gather | solution.py:71
  461.6 3.3 fusion
  465.8 8.7 stack.2
  474.5 7.6 all-to-all-start
  482.2 4.9 convert_reduce_fusion
  487.2 405.4 %all-to-all-done = bf16[32,384,1024]{2,1,0:T(8,128)(2,1)} async-done(((bf16[32,384,1024]{2,1,0:T(8,128)(2,1)}), bf16[32,384,1024]{2,1,0:T(8,128)(2,1)}, u32[]{:S(2)}, u32[]{:S(2)}) %all-to-all-start) | async-done | bytes 25165856 | tf_op jit(solution)/shard_map/all_to_all | solution.py:78
  892.6 10.7 %convolution_divide_fusion = f32[8,1024]{1,0:T(8,128)} fusion(bf16[12288,1024]{1,0:T(8,128)(2,1)} %bitcast.30, bf16[8,12288]{1,0:T(8,128)(2,1)S(1)} %convert_reduce_fusion, f32[8]{0:T(128)S(1)} %convert_reduce_fusion.1), kind=kOutput, calls=%fused_computation.64 | convolution fusion | flops 201334784 | bytes 25395232 | tf_op jit(solution)/shard_map/dot_general | solution.py:81
  (119 shorter events, 82.9 us)
Async XLA Ops:
  7.2 454.4 %copy-start = (bf16[1536,1024]{1,0:T(8,128)(2,1)S(1)}, bf16[1536,1024]{1,0:T(8,128)(2,1)}, u32[]{:S(2)}) copy-start(bf16[1536,1024]{1,0:T(8,128)(2,1)} %param.13) | copy-start | bytes 9437188
  7.2 30.0 %all-gather.8.cloned.1.call-start = ((), (), s32[]{:S(2)}) async-start(), calls=%async_computation.7 | async-start | bytes 1474560 | tf_op jit(solution)/shard_map/all_gather | solution.py:35
  7.9 70.7 %reduce-scatter.19.cloned.1.call-start = ((), (), s32[]{:S(2)}) async-start(), calls=%async_computation.14 | async-start | bytes 1474560
  38.0 6.3 collective-permute-start.1
  39.9 6.8 collective-permute-start
  53.0 27.5 %copy-start.7 = (bf16[384,384]{1,0:T(8,128)(2,1)S(1)}, bf16[384,384]{1,0:T(8,128)(2,1)}, u32[]{:S(2)}) copy-start(bf16[384,384]{1,0:T(8,128)(2,1)} %param.8) | copy-start | bytes 884740
  53.0 54.2 %all-gather.10.cloned.1.call-start = ((), (), s32[]{:S(2)}) async-start(), calls=%async_computation.8 | async-start | bytes 1474560 | tf_op jit(solution)/shard_map/all_gather | solution.py:35
  82.2 67.2 %reduce-scatter.21.cloned.1.call-start = ((), (), s32[]{:S(2)}) async-start(), calls=%async_computation.15 | async-start | bytes 1474560
  108.0 7.0 collective-permute-start.3
  109.9 7.5 collective-permute-start.2
  123.8 27.5 %copy-start.6 = (bf16[384,384]{1,0:T(8,128)(2,1)S(1)}, bf16[384,384]{1,0:T(8,128)(2,1)}, u32[]{:S(2)}) copy-start(bf16[384,384]{1,0:T(8,128)(2,1)} %add_convert_fusion.5) | copy-start | bytes 884740
  123.8 54.1 %all-gather.12.cloned.1.call-start = ((), (), s32[]{:S(2)}) async-start(), calls=%async_computation.9 | async-start | bytes 1474560 | tf_op jit(solution)/shard_map/all_gather | solution.py:35
  153.0 67.1 %reduce-scatter.23.cloned.1.call-start = ((), (), s32[]{:S(2)}) async-start(), calls=%async_computation.16 | async-start | bytes 1474560
  178.8 7.0 collective-permute-start.5
  180.7 7.4 collective-permute-start.4
  194.5 27.5 %copy-start.3 = (bf16[384,384]{1,0:T(8,128)(2,1)S(1)}, bf16[384,384]{1,0:T(8,128)(2,1)}, u32[]{:S(2)}) copy-start(bf16[384,384]{1,0:T(8,128)(2,1)} %add_convert_fusion.4) | copy-start | bytes 884740
  194.5 54.1 %all-gather.14.cloned.1.call-start = ((), (), s32[]{:S(2)}) async-start(), calls=%async_computation.10 | async-start | bytes 1474560 | tf_op jit(solution)/shard_map/all_gather | solution.py:35
  223.8 67.1 %reduce-scatter.25.cloned.1.call-start = ((), (), s32[]{:S(2)}) async-start(), calls=%async_computation.17 | async-start | bytes 1474560
  249.6 7.0 collective-permute-start.7
  251.5 7.5 collective-permute-start.6
  265.3 27.5 %copy-start.4 = (bf16[384,384]{1,0:T(8,128)(2,1)S(1)}, bf16[384,384]{1,0:T(8,128)(2,1)}, u32[]{:S(2)}) copy-start(bf16[384,384]{1,0:T(8,128)(2,1)} %add_convert_fusion.3) | copy-start | bytes 884740
  265.3 54.1 %all-gather.16.cloned.1.call-start = ((), (), s32[]{:S(2)}) async-start(), calls=%async_computation.11 | async-start | bytes 1474560 | tf_op jit(solution)/shard_map/all_gather | solution.py:35
  294.5 67.5 %reduce-scatter.27.cloned.1.call-start = ((), (), s32[]{:S(2)}) async-start(), calls=%async_computation.18 | async-start | bytes 1474560
  320.4 7.3 collective-permute-start.9
  322.5 7.6 collective-permute-start.8
  336.5 54.1 %all-gather.18.cloned.1.call-start = ((), (), s32[]{:S(2)}) async-start(), calls=%async_computation.12 | async-start | bytes 1474560 | tf_op jit(solution)/shard_map/all_gather | solution.py:35
  365.7 67.4 %reduce-scatter.29.cloned.1.call-start = ((), (), s32[]{:S(2)}) async-start(), calls=%async_computation.19 | async-start | bytes 1474560
  391.6 7.2 collective-permute-start.11
  393.7 7.5 collective-permute-start.10
  407.5 29.2 %copy-start.14 = (bf16[1024]{0:T(1024)(128)(2,1)S(1)}, bf16[1024]{0:T(1024)(128)(2,1)}, u32[]{:S(2)}) copy-start(bf16[1024]{0:T(1024)(128)(2,1)} %param.14) | copy-start | bytes 6148
  407.5 54.1 %all-gather.20.cloned.1.call-start = ((), (), s32[]{:S(2)}) async-start(), calls=%async_computation.13 | async-start | bytes 1474560 | tf_op jit(solution)/shard_map/all_gather | solution.py:71
  474.5 418.1 %all-to-all-start = ((bf16[32,384,1024]{2,1,0:T(8,128)(2,1)}), bf16[32,384,1024]{2,1,0:T(8,128)(2,1)}, u32[]{:S(2)}, u32[]{:S(2)}) async-start(bf16[32,384,1024]{2,1,0:T(8,128)(2,1)} %stack.2), calls=%async_computation | async-start | bytes 50331648 | tf_op jit(solution)/shard_map/all_to_all | solution.py:78
  (12 other events, 120.2 us)
Sparse Core Ops, SparseCore 0:
  9.7 27.4 all-gather.7
  53.1 25.4 reduce-scatter.18
  82.3 24.7 all-gather.9
  123.9 25.4 reduce-scatter.20
  153.1 24.7 all-gather.11
  194.6 25.4 reduce-scatter.22
  223.9 24.7 all-gather.13
  265.4 25.4 reduce-scatter.24
  294.6 24.7 all-gather.15
  336.6 25.4 reduce-scatter.26
  365.8 24.7 all-gather.17
  407.6 25.4 reduce-scatter.28
  436.8 24.7 all-gather.19
